TPU v7x, 32 devices: a whole 2x2x4 slice. The times are simulated.
32 devices in a mesh: dp: 8 (over y, x, core), tensor: 4 (over z).
Axes of the slice: x: 2, y: 2, z: 4, core: 2. Of those that a mesh axis runs over, the one named last changes fastest.
Arguments:
- inputs: bfloat16 [6144, 2048], P('dp', 'tensor'), may hold values from -6 to 6
- labels: int32 [6144], P('dp'), may hold values from 0 to 1
- cotangent: bfloat16 [6144, 2048], P('dp', 'tensor'), may hold values from -6 to 6
- gate_weight: bfloat16 [2048, 2], P('tensor'), may hold values from -0.125 to 0.125
- weight_in: bfloat16 [3, 2048, 4096], P(None, None, 'tensor'), may hold values from -0.125 to 0.125
- weight_out: bfloat16 [3, 4096, 2048], P(None, 'tensor'), may hold values from -0.09375 to 0.09375
Outputs:
- input_grad: float32 [6144, 2048], P('dp', 'tensor')
- gate_grad: float32 [2048, 2], P('tensor')
- weight_in_grad: float32 [3, 2048, 4096], P(None, 'dp', 'tensor')
- weight_out_grad: float32 [3, 4096, 2048], P(None, 'tensor', 'dp')
All inputs are finite; a program needn't handle non-finite values.
Results may differ from a plain program's by a relative error of at most 0.0075.
Values may be sent and summed in bfloat16 or wider, within the bound.
A program may use at most 192 MiB of HBM per device.

v0:
```python
import jax
import jax.numpy as jnp
from jax import lax
from jax.sharding import PartitionSpec as P


def expert_grads(x_full, hidden_grad, active, share, cot_float):
    contract_rows = (((0,), (0,)), ((), ()))
    out_grad = (share * cot_float).astype(jnp.bfloat16)
    grad_one = lax.dot_general(
        x_full, hidden_grad, contract_rows, preferred_element_type=jnp.float32
    )
    grad_two = lax.dot_general(active, out_grad, contract_rows, preferred_element_type=jnp.float32)
    return (grad_one, grad_two)


def shards(inputs, labels, cotangent, gate_weight, weight_in, weight_out):
    contract_cols = (((1,), (1,)), ((), ()))
    num_tasks = gate_weight.shape[1]
    num_experts = weight_in.shape[0]
    x_full, cot_full = (
        lax.all_gather(inputs, "tensor", axis=1, tiled=True),
        lax.all_gather(cotangent, "tensor", axis=1, tiled=True),
    )
    logits = lax.psum(jnp.dot(inputs, gate_weight, preferred_element_type=jnp.float32), "tensor")
    picked = (labels[:, None] == jnp.arange(num_tasks, dtype=jnp.int32)[None, :]).astype(
        jnp.float32
    )
    task_gate = jax.nn.sigmoid(jnp.sum(logits * picked, axis=1))
    mixing = jnp.concatenate([(1.0 - task_gate)[:, None], task_gate[:, None] * picked], axis=1)
    cot_float = cot_full.astype(jnp.float32)
    scores = []
    actives = []
    hidden_grads = []
    grads_in = []
    grads_out = []
    partial_input = None
    for expert in range(num_experts):
        hidden = jnp.dot(x_full, weight_in[expert], preferred_element_type=jnp.float32)
        sigma = jax.nn.sigmoid(hidden)
        active = (hidden * sigma).astype(jnp.bfloat16)
        back_grad = lax.dot_general(
            cot_full, weight_out[expert], contract_cols, preferred_element_type=jnp.float32
        )
        scores.append(jnp.sum(active.astype(jnp.float32) * back_grad, axis=1))
        share = mixing[:, expert : expert + 1]
        hidden_grad = (share * back_grad * sigma * (1.0 + hidden * (1.0 - sigma))).astype(
            jnp.bfloat16
        )
        term = lax.dot_general(
            hidden_grad, weight_in[expert], contract_cols, preferred_element_type=jnp.float32
        )
        partial_input = term if partial_input is None else partial_input + term
        actives.append(active)
        hidden_grads.append(hidden_grad)
        grad_one, grad_two = expert_grads(x_full, hidden_grad, active, share, cot_float)
        grads_in.append(grad_one)
        grads_out.append(grad_two)
    score = lax.psum(jnp.stack(scores, axis=1), "tensor")
    own = jnp.sum(score[:, 1:] * picked, axis=1) - score[:, 0]
    slope = task_gate * (1.0 - task_gate) * own
    slope_rows = slope[:, None] * picked
    input_grad = lax.psum_scatter(partial_input, "tensor", scatter_dimension=1, tiled=True)
    input_grad = input_grad + jnp.dot(
        slope_rows, gate_weight.astype(jnp.float32).T, precision=lax.Precision.HIGHEST
    )
    gate_part = jnp.dot(inputs.astype(jnp.float32).T, slope_rows, precision=lax.Precision.HIGHEST)
    gate_grad = lax.psum(gate_part, "dp")
    weight_in_grad, weight_out_grad = (
        lax.psum_scatter(jnp.stack(grads_in), "dp", scatter_dimension=1, tiled=True),
        lax.psum_scatter(jnp.stack(grads_out), "dp", scatter_dimension=2, tiled=True),
    )
    return (input_grad, gate_grad, weight_in_grad, weight_out_grad)


def solution(mesh):
    in_specs = (
        P("dp", "tensor"),
        P("dp"),
        P("dp", "tensor"),
        P("tensor", None),
        P(None, None, "tensor"),
        P(None, "tensor", None),
    )
    out_specs = (
        P("dp", "tensor"),
        P("tensor", None),
        P(None, "dp", "tensor"),
        P(None, "tensor", "dp"),
    )
    return jax.shard_map(shards, mesh=mesh, in_specs=in_specs, out_specs=out_specs, check_vma=False)
```

profile of v0, /device:TPU:0, one launch (start us, length us, event | category | flops | bytes accessed | tf_op | source)
XLA Modules:
  0.0 653.9 jit_solution(352505402512204216)
XLA Ops:
  7.2 0.0 copy-start
  7.2 0.0 all-gather.5.cloned.1.call-start
  7.2 0.7 all-gather.5.cloned.1.call-update
  7.9 0.0 all-gather.3.cloned.1.call-start
  8.0 0.7 all-gather.3.cloned.1.call-update
  8.7 0.0 reduce-scatter.4.cloned.1.call-start
  8.7 0.0 copy-done
  8.7 1.4 fusion.52
  10.1 65.6 %all-gather.5.cloned.1.call-done = bf16[768,2048]{1,0:T(8,128)(2,1)} async-done(((bf16[768,512]{1,0:T(8,128)(2,1)}), bf16[768,2048]{1,0:T(8,128)(2,1)}) %all-gather.5.cloned.1.call-update) | async-done | bytes 3145744 | tf_op jit(solution)/shard_map/all_gather | solution.py:22
  75.8 6.1 fusion.17
  81.9 57.6 %all-gather.3.cloned.1.call-done = bf16[768,2048]{1,0:T(8,128)(2,1)} async-done(((bf16[768,512]{1,0:T(8,128)(2,1)}), bf16[768,2048]{1,0:T(8,128)(2,1)}) %all-gather.3.cloned.1.call-update) | async-done | bytes 3145744 | tf_op jit(solution)/shard_map/all_gather | solution.py:23
  139.4 8.6 %multiply_reduce_fusion.2 = (f32[768]{0:T(1024)S(1)}, f32[768,1024]{1,0:T(8,128)}) fusion(f32[768,1024]{1,0:T(8,128)S(1)} %fusion.17, bf16[768,2048]{1,0:T(8,128)(2,1)} %all-gather.3.cloned.1.call-done, bf16[3,1024,2048]{2,1,0:T(8,128)(2,1)} %param.11), kind=kOutput, calls=%fused_computation.49 | convolution fusion | flops 3227516160 | bytes 13634560 | tf_op jit(solution)/shard_map/dot_general | solution.py:42
  148.0 0.0 copy-done.14
  148.1 0.0 copy-start.12
  148.1 5.3 fusion.11
  153.4 0.0 slice-done
  153.4 0.0 slice-done.1
  153.4 0.0 slice-done.2
  153.4 0.0 copy-done.12
  153.5 0.0 copy-start.2
  153.5 5.3 multiply_reduce_fusion.1
  158.8 5.7 fusion.5
  164.5 0.0 copy-start.3
  164.5 0.0 copy-start.11
  164.5 5.3 multiply_reduce_fusion
  169.9 16.4 %all-reduce = (f32[768,3]{0,1:T(4,128)S(1)}, f32[768,2]{0,1:T(2,128)S(1)}) all-reduce(f32[768,3]{0,1:T(4,128)S(1)} %pad_maximum_fusion.2, f32[768,2]{0,1:T(2,128)S(1)} %fusion.52), channel_id=1, replica_groups=mesh['dp'=8,'tensor'=4] {'tensor'}, use_global_device_ids=true, to_apply=%region_6.0 | all-reduce | flops 3840 | bytes 30720 | tf_op jit(solution)/shard_map/psum | solution.py:59
  186.2 0.0 copy-done.11
  186.3 0.0 slice-start.3
  186.3 0.0 slice-start.4
  186.3 6.0 multiply_convert_fusion.3
  192.4 0.0 copy-start.6
  192.4 0.0 copy-start.8
  192.4 0.0 slice-start.5
  192.4 8.7 %fusion.3 = f32[768,2048]{1,0:T(8,128)} fusion(bf16[768,1024]{1,0:T(8,128)(2,1)S(1)} %get-tuple-element.22, bf16[3,2048,1024]{2,1,0:T(8,128)(2,1)} %param.10), kind=kOutput, calls=%fused_computation.15 | convolution fusion | flops 3221225472 | bytes 12058624 | tf_op jit(solution)/shard_map/dot_general | solution.py:50
  201.1 0.0 copy-done.8
  201.1 5.4 fusion.9
  206.6 1.3 multiply_convert_fusion.5
  207.9 1.1 copy-done.10
  209.0 8.3 %add_add_fusion = f32[768,2048]{1,0:T(8,128)} fusion(f32[768,2048]{1,0:T(8,128)} %fusion.3, f32[768,2048]{1,0:T(8,128)} %fusion.9, bf16[768,1024]{1,0:T(8,128)(2,1)S(1)} %multiply_convert_fusion.5, bf16[3,2048,1024]{2,1,0:T(8,128)(2,1)S(1)} %bitcast.74), kind=kOutput, calls=%fused_computation.8 | convolution fusion | flops 3224371200 | bytes 24641536 | tf_op jit(solution)/shard_map/dot_general | solution.py:50
  217.3 0.0 reduce-scatter.4.cloned.1.call-update
  217.3 0.2 reduce-scatter.6.cloned.1.call-start
  217.5 0.0 copy-start.9
  217.5 6.1 convolution_bitcast_fusion.5
  223.6 0.0 copy-start.7
  223.6 3.5 convolution_bitcast_fusion.4
  227.2 3.6 convolution_bitcast_fusion.3
  230.8 9.0 %pad_maximum_fusion = f32[3,2048,1024]{1,2,0:T(8,128)} fusion(f32[1,2048,1024]{1,2,0:T(8,128)S(1)} %convolution_bitcast_fusion.3, f32[1,2048,1024]{1,2,0:T(8,128)S(1)} %convolution_bitcast_fusion.4, f32[1,2048,1024]{1,2,0:T(8,128)S(1)} %convolution_bitcast_fusion.5), kind=kLoop, calls=%fused_computation | loop fusion | flops 12582912 | bytes 50331648 | tf_op jit(solution)/shard_map/stack | solution.py:70
  239.7 0.0 reduce-scatter.6.cloned.1.call-update
  239.7 0.3 reduce-scatter.8.cloned.1.call-start
  240.0 0.0 copy-start.4
  240.0 0.0 copy-start.13
  240.0 6.7 %convolution_bitcast_fusion.1 = f32[1,1024,2048]{2,1,0:T(8,128)S(1)} fusion(bf16[768,2048]{1,0:T(8,128)(2,1)} %all-gather.3.cloned.1.call-done, f32[768]{0:T(1024)S(1)} %get-tuple-element.8, f32[768,1024]{1,0:T(8,128)} %copy-done.2), kind=kOutput, calls=%fused_computation.10 | convolution fusion | flops 3229876224 | bytes 14683136 | tf_op jit(solution)/shard_map/dot_general | solution.py:13
  246.7 3.7 convolution_bitcast_fusion
  250.4 3.7 convolution_bitcast_fusion.2
  254.2 8.7 %pad_maximum_fusion.1 = f32[3,1024,2048]{2,1,0:T(8,128)} fusion(f32[1,1024,2048]{2,1,0:T(8,128)S(1)} %convolution_bitcast_fusion, f32[1,1024,2048]{2,1,0:T(8,128)S(1)} %convolution_bitcast_fusion.1, f32[1,1024,2048]{2,1,0:T(8,128)S(1)} %convolution_bitcast_fusion.2), kind=kLoop, calls=%fused_computation.1 | loop fusion | flops 12582912 | bytes 50331648 | tf_op jit(solution)/shard_map/stack | solution.py:71
  262.9 0.0 reduce-scatter.8.cloned.1.call-update
  262.9 1.1 copy-done.1
  264.0 0.4 convolution_bitcast_fusion.6
  264.4 12.8 %psum.23 = f32[512,2]{0,1:T(2,128)} all-reduce(f32[512,2]{0,1:T(2,128)S(1)} %convolution_bitcast_fusion.6), channel_id=1, replica_groups=mesh['dp'=8,'tensor'=4] {'dp'}, use_global_device_ids=true, to_apply=%region_8.0 | all-reduce | flops 1024 | bytes 8192 | tf_op jit(solution)/shard_map/psum | solution.py:68
  277.2 49.9 %reduce-scatter.4.cloned.1.call-done = f32[768,512]{1,0:T(8,128)} async-done(((f32[768,2048]{1,0:T(8,128)}), f32[768,512]{1,0:T(8,128)}) %reduce-scatter.4.cloned.1.call-update) | async-done | bytes 1572880 | tf_op jit(solution)/shard_map/reduce_scatter | solution.py:63
  327.1 3.4 convolution_add_fusion
  330.5 156.6 %reduce-scatter.6.cloned.1.call-done = f32[3,256,1024]{1,2,0:T(8,128)} async-done(((f32[3,2048,1024]{1,2,0:T(8,128)}), f32[3,256,1024]{1,2,0:T(8,128)}) %reduce-scatter.6.cloned.1.call-update) | async-done | bytes 3145744 | tf_op jit(solution)/shard_map/reduce_scatter | solution.py:70
  487.1 3.5 copy.10
  490.6 156.5 %reduce-scatter.8.cloned.1.call-done = f32[3,1024,256]{2,1,0:T(8,128)} async-done(((f32[3,1024,2048]{2,1,0:T(8,128)}), f32[3,1024,256]{2,1,0:T(8,128)}) %reduce-scatter.8.cloned.1.call-update) | async-done | bytes 3145744 | tf_op jit(solution)/shard_map/reduce_scatter | solution.py:71
  (31 shorter events, 0.1 us)
Async XLA Ops:
  7.2 1.5 copy-start
  7.2 68.6 %all-gather.5.cloned.1.call-start = ((), (), s32[]{:S(2)}) async-start(), calls=%async_computation.4 | async-start | bytes 3932160 | tf_op jit(solution)/shard_map/all_gather | solution.py:22
  7.9 131.5 %all-gather.3.cloned.1.call-start = ((), (), s32[]{:S(2)}) async-start(), calls=%async_computation.3 | async-start | bytes 3932160 | tf_op jit(solution)/shard_map/all_gather | solution.py:23
  8.7 318.4 %reduce-scatter.4.cloned.1.call-start = ((), (), s32[]{:S(2)}) async-start(), calls=%async_computation.5 | async-start | bytes 7864320 | tf_op jit(solution)/shard_map/reduce_scatter | solution.py:63
  139.4 8.6 %copy-start.14 = (bf16[768,2048]{1,0:T(8,128)(2,1)S(1)}, bf16[768,2048]{1,0:T(8,128)(2,1)}, u32[]{:S(2)}) copy-start(bf16[768,2048]{1,0:T(8,128)(2,1)} %all-gather.5.cloned.1.call-done) | copy-start | bytes 9437188
  139.4 14.0 %slice-start = ((s8[12582912]{0:T(1024)(128)(4,1)}), s8[4194304]{0:T(1024)(128)(4,1)S(1)}, s32[]{:S(2)}) async-start(s8[12582912]{0:T(1024)(128)(4,1)} %bitcast.71), calls=%async_computation.8 | async-start | bytes 8388608
  139.4 14.0 %slice-start.1 = ((s8[12582912]{0:T(1024)(128)(4,1)}), s8[4194304]{0:T(1024)(128)(4,1)S(1)}, s32[]{:S(2)}) async-start(s8[12582912]{0:T(1024)(128)(4,1)} %bitcast.71), calls=%async_computation.9 | async-start | bytes 8388608
  148.0 5.4 slice-start.2
  148.1 5.4 copy-start.12
  153.5 5.3 copy-start.2
  164.5 5.4 copy-start.3
  164.5 21.8 %copy-start.11 = (s32[768]{0:T(1024)S(1)}, s32[768]{0:T(1024)}, u32[]{:S(2)}) copy-start(s32[768]{0:T(1024)} %param.7) | copy-start | bytes 9220
  186.3 14.8 %slice-start.3 = ((s8[12582912]{0:T(1024)(128)(4,1)}), s8[4194304]{0:T(1024)(128)(4,1)S(1)}, s32[]{:S(2)}) async-start(s8[12582912]{0:T(1024)(128)(4,1)} %bitcast.73), calls=%async_computation.11 | async-start | bytes 8388608
  186.3 14.8 %slice-start.4 = ((s8[12582912]{0:T(1024)(128)(4,1)}), s8[4194304]{0:T(1024)(128)(4,1)S(1)}, s32[]{:S(2)}) async-start(s8[12582912]{0:T(1024)(128)(4,1)} %bitcast.73), calls=%async_computation.12 | async-start | bytes 8388608
  192.4 8.7 %copy-start.6 = (bf16[768,1024]{1,0:T(8,128)(2,1)}, bf16[768,1024]{1,0:T(8,128)(2,1)S(1)}, u32[]{:S(2)}) copy-start(bf16[768,1024]{1,0:T(8,128)(2,1)S(1)} %get-tuple-element.22) | copy-start | bytes 4718596
  192.4 8.7 %copy-start.8 = (bf16[768,1024]{1,0:T(8,128)(2,1)}, bf16[768,1024]{1,0:T(8,128)(2,1)S(1)}, u32[]{:S(2)}) copy-start(bf16[768,1024]{1,0:T(8,128)(2,1)S(1)} %get-tuple-element.23) | copy-start | bytes 4718596
  192.4 8.7 %slice-start.5 = ((s8[12582912]{0:T(1024)(128)(4,1)}), s8[4194304]{0:T(1024)(128)(4,1)S(1)}, s32[]{:S(2)}) async-start(s8[12582912]{0:T(1024)(128)(4,1)} %bitcast.73), calls=%async_computation.13 | async-start | bytes 8388608
  201.1 5.4 copy-start.5
  207.8 1.1 copy-start.10
  217.3 269.8 %reduce-scatter.6.cloned.1.call-start = ((), (), s32[]{:S(2)}) async-start(), calls=%async_computation.6 | async-start | bytes 28311552 | tf_op jit(solution)/shard_map/reduce_scatter | solution.py:70
  217.5 6.1 copy-start.9
  217.5 6.1 copy-start.15
  223.6 3.6 copy-start.7
  239.7 407.4 %reduce-scatter.8.cloned.1.call-start = ((), (), s32[]{:S(2)}) async-start(), calls=%async_computation.7 | async-start | bytes 28311552 | tf_op jit(solution)/shard_map/reduce_scatter | solution.py:71
  240.0 6.7 %copy-start.4 = (f32[768,1024]{1,0:T(8,128)S(1)}, f32[768,1024]{1,0:T(8,128)}, u32[]{:S(2)}) copy-start(f32[768,1024]{1,0:T(8,128)} %copy-done.3) | copy-start | bytes 9437188
  240.0 6.7 %copy-start.13 = (bf16[768,2048]{1,0:T(8,128)(2,1)S(1)}, bf16[768,2048]{1,0:T(8,128)(2,1)}, u32[]{:S(2)}) copy-start(bf16[768,2048]{1,0:T(8,128)(2,1)} %all-gather.3.cloned.1.call-done) | copy-start | bytes 9437188
  262.9 1.1 copy-start.1
Sparse Core Ops, SparseCore 0:
  9.6 66.1 all-gather.4
  77.3 62.0 all-gather.2
  217.4 109.6 reduce-scatter.3
  330.5 156.5 reduce-scatter.5
  491.1 155.9 reduce-scatter.7
where the time goes:
time: 661 us; the launch traced here: 654 us
  waiting for transfers between devices  488 us (74%)
  matrix products  91.3 us (14%)
  blocking collectives  29.1 us (4%)
  other arithmetic  25 us (4%)
  between operations  14.4 us (2%)
    reduce_scatter x1, waiting for transfers between devices, shards(): lax.psum_scatter(jnp.stack(grads_in), 'dp', scatter_dimension=1, tiled=True)  157 us
    reduce_scatter x1, waiting for transfers between devices, shards(): lax.psum_scatter(jnp.stack(grads_out), 'dp', scatter_dimension=2, tiled=T...  157 us
    all_gather x1, waiting for transfers between devices, shards(): lax.all_gather(inputs, 'tensor', axis=1, tiled=True)  65.6 us
    all_gather x1, waiting for transfers between devices, shards(): lax.all_gather(cotangent, 'tensor', axis=1, tiled=True)  57.6 us
    reduce_scatter x1, waiting for transfers between devices, shards(): lax.psum_scatter(partial_input, 'tensor', scatter_dimension=1, tiled=True)  49.9 us
    dot_general x3, matrix products, shards(): lax.dot_general(hidden_grad, weight_in[expert], contract_cols, preferred_...  22.4 us
    dot_general x3, matrix products, shards(): lax.dot_general(cot_full, weight_out[expert], contract_cols, preferred_el...  19.2 us
    dot_general x3, matrix products, shards(): jnp.dot(x_full, weight_in[expert], preferred_element_type=jnp.float32)  17.1 us
  transfers between devices with their start and end apart: 5, of which 5 were waited for; matrix products, arithmetic and copies ran while one was open for 9% of the time, Pallas kernels for 0%

commit v1 on v0

--- a/solution.py
+++ b/solution.py
@@ -2,6 +2,23 @@
 import jax.numpy as jnp
 from jax import lax
 from jax.sharding import PartitionSpec as P
+
+
+def in_order(pieces, dim):
+    pieces = jnp.moveaxis(pieces, 0, dim)
+    shape = pieces.shape
+    return pieces.reshape(*shape[:dim], shape[dim] * shape[dim + 1], *shape[dim + 2 :])
+
+
+def gather_around(array, axis, dim):
+    size = lax.axis_size(axis)
+    upward = [(i, (i + 1) % size) for i in range(size)]
+    blocks = [array]
+    while len(blocks) < size:
+        blocks.append(lax.ppermute(blocks[-1], axis, upward))
+    place = lax.axis_index(axis)
+    blocks = jnp.stack(blocks)[(place - jnp.arange(size)) % size]
+    return in_order(blocks, dim)
 
 
 def expert_grads(x_full, hidden_grad, active, share, cot_float):
@@ -20,7 +37,7 @@
     num_experts = weight_in.shape[0]
     x_full, cot_full = (
         lax.all_gather(inputs, "tensor", axis=1, tiled=True),
-        lax.all_gather(cotangent, "tensor", axis=1, tiled=True),
+        gather_around(cotangent, "tensor", 1),
     )
     logits = lax.psum(jnp.dot(inputs, gate_weight, preferred_element_type=jnp.float32), "tensor")
     picked = (labels[:, None] == jnp.arange(num_tasks, dtype=jnp.int32)[None, :]).astype(

time: 661 us -> 654 us (0.989)
  waiting for transfers between devices: 488 us -> 445 us
  starting transfers between devices: 0.58 us -> 25.4 us
  local copies, waits for them, and re-layouts: 5.88 us -> 13.8 us
    ppermute x0 -> x3, waiting for transfers between devices: none -> 81.1 us  [gather_around(): blocks.append(lax.ppermute(blocks[-1], axis, upward))]
    all_gather x1, waiting for transfers between devices: 65.6 us -> 0.01 us  [shards(): lax.all_gather(inputs, 'tensor', axis=1, tiled=True)]
    all_gather x1 -> x0, waiting for transfers between devices: 57.6 us -> none  [shards(): lax.all_gather(cotangent, 'tensor', axis=1, tiled=True)]
    ppermute x0 -> x3, starting transfers between devices: none -> 24.8 us  [gather_around(): blocks.append(lax.ppermute(blocks[-1], axis, upward))]
  transfers between devices with their start and end apart: 5 -> 7, of which waited for: 5 -> 6; matrix products, arithmetic and copies ran while one was open for 9% -> 10% of each run, Pallas kernels for 0% -> 0%
where the time goes in v1:
time: 654 us; the launch traced here: 646 us
  waiting for transfers between devices  445 us (68%)
  matrix products  90.3 us (14%)
  blocking collectives  29.8 us (5%)
  other arithmetic  26.7 us (4%)
  starting transfers between devices  25.4 us (4%)
  between operations  14.4 us (2%)
  local copies, waits for them, and re-layouts  13.8 us (2%)
    reduce_scatter x1, waiting for transfers between devices, shards(): lax.psum_scatter(jnp.stack(grads_in), 'dp', scatter_dimension=1, tiled=True)  157 us
    reduce_scatter x1, waiting for transfers between devices, shards(): lax.psum_scatter(jnp.stack(grads_out), 'dp', scatter_dimension=2, tiled=T...  157 us
    ppermute x3, waiting for transfers between devices, gather_around(): blocks.append(lax.ppermute(blocks[-1], axis, upward))  81.1 us
    reduce_scatter x1, waiting for transfers between devices, shards(): lax.psum_scatter(partial_input, 'tensor', scatter_dimension=1, tiled=True)  50 us
    ppermute x3, starting transfers between devices, gather_around(): blocks.append(lax.ppermute(blocks[-1], axis, upward))  24.8 us
    dot_general x3, matrix products, shards(): lax.dot_general(hidden_grad, weight_in[expert], contract_cols, preferred_...  22.2 us
    dot_general x3, matrix products, shards(): lax.dot_general(cot_full, weight_out[expert], contract_cols, preferred_el...  18.6 us
    dot_general x3, matrix products, shards(): jnp.dot(x_full, weight_in[expert], preferred_element_type=jnp.float32)  17.3 us
  transfers between devices with their start and end apart: 7, of which 6 were waited for; matrix products, arithmetic and copies ran while one was open for 10% of the time, Pallas kernels for 0%

profile of v1, /device:TPU:0, one launch (start us, length us, event | category | flops | bytes accessed | tf_op | source)
XLA Modules:
  0.0 645.5 jit_solution(8803901157916880136)
XLA Ops:
  7.2 0.0 copy-start
  7.2 0.0 all-gather.2.cloned.1.call-start
  7.2 0.7 all-gather.2.cloned.1.call-update
  7.9 0.0 reduce-scatter.4.cloned.1.call-start
  8.0 3.1 collective-permute-start
  11.1 26.7 %collective-permute-done = bf16[768,512]{1,0:T(8,128)(2,1)S(1)} collective-permute-done((bf16[768,512]{1,0:T(8,128)(2,1)}, bf16[768,512]{1,0:T(8,128)(2,1)S(1)}, u32[]{:S(2)}, u32[]{:S(2)}) %collective-permute-start) | collective-permute-done | bytes 786464 | tf_op jit(solution)/shard_map/ppermute | solution.py:18
  37.8 6.9 %collective-permute-start.1 = (bf16[768,512]{1,0:T(8,128)(2,1)S(1)}, bf16[768,512]{1,0:T(8,128)(2,1)S(1)}, u32[]{:S(2)}, u32[]{:S(2)}) collective-permute-start(bf16[768,512]{1,0:T(8,128)(2,1)S(1)} %collective-permute-done), channel_id=1, source_target_pairs={{0,1},{1,2},{2,3},{3,0},{4,5},{5,6},{6,7},{7,4},{8,9},{9,10},{10,1... | collective-permute-start | bytes 2359304 | tf_op jit(solution)/shard_map/ppermute | solution.py:18
  44.7 38.8 %collective-permute-done.1 = bf16[768,512]{1,0:T(8,128)(2,1)S(1)} collective-permute-done((bf16[768,512]{1,0:T(8,128)(2,1)S(1)}, bf16[768,512]{1,0:T(8,128)(2,1)S(1)}, u32[]{:S(2)}, u32[]{:S(2)}) %collective-permute-start.1) | collective-permute-done | bytes 786464 | tf_op jit(solution)/shard_map/ppermute | solution.py:18
  83.5 14.8 %collective-permute-start.2 = (bf16[768,512]{1,0:T(8,128)(2,1)S(1)}, bf16[768,512]{1,0:T(8,128)(2,1)S(1)}, u32[]{:S(2)}, u32[]{:S(2)}) collective-permute-start(bf16[768,512]{1,0:T(8,128)(2,1)S(1)} %collective-permute-done.1), channel_id=1, source_target_pairs={{0,1},{1,2},{2,3},{3,0},{4,5},{5,6},{6,7},{7,4},{8,9},{9,10},{10,1... | collective-permute-start | bytes 2359304 | tf_op jit(solution)/shard_map/ppermute | solution.py:18
  98.3 1.4 fusion.54
  99.7 15.7 %collective-permute-done.2 = bf16[768,512]{1,0:T(8,128)(2,1)S(1)} collective-permute-done((bf16[768,512]{1,0:T(8,128)(2,1)S(1)}, bf16[768,512]{1,0:T(8,128)(2,1)S(1)}, u32[]{:S(2)}, u32[]{:S(2)}) %collective-permute-start.2) | collective-permute-done | bytes 786464 | tf_op jit(solution)/shard_map/ppermute | solution.py:18
  115.4 0.0 copy-done.13
  115.4 0.9 copy-done.15
  116.3 2.0 pad_maximum_fusion.2
  118.3 2.4 gather_fusion
  120.8 4.6 copy.12
  125.4 6.3 fusion.17
  131.7 0.0 slice-start
  131.7 0.0 slice-start.1
  131.7 7.8 %multiply_reduce_fusion.2 = (f32[768]{0:T(1024)S(1)}, f32[768,1024]{1,0:T(8,128)}) fusion(f32[768,1024]{1,0:T(8,128)S(1)} %fusion.17, bf16[768,2048]{0,1:T(8,128)(2,1)S(1)} %bitcast.81, bf16[3,1024,2048]{2,1,0:T(8,128)(2,1)} %param.11), kind=kOutput, calls=%fused_computation.51 | convolution fusion | flops 3227516160 | bytes 13634560 | tf_op jit(solution)/shard_map/dot_general | solution.py:59
  139.5 5.3 fusion.11
  144.9 5.4 multiply_reduce_fusion.1
  150.3 5.7 fusion.5
  156.0 0.0 copy-start.3
  156.0 0.0 copy-start.16
  156.0 5.4 multiply_reduce_fusion
  161.5 17.0 %all-reduce = (f32[768,3]{0,1:T(4,128)S(1)}, f32[768,2]{0,1:T(2,128)S(1)}) all-reduce(f32[768,3]{0,1:T(4,128)S(1)} %pad_maximum_fusion.3, f32[768,2]{0,1:T(2,128)S(1)} %fusion.54), channel_id=1, replica_groups=mesh['dp'=8,'tensor'=4] {'tensor'}, use_global_device_ids=true, to_apply=%region_6.7 | all-reduce | flops 3840 | bytes 30720 | tf_op jit(solution)/shard_map/psum | solution.py:76
  178.6 0.0 slice-start.3
  178.6 0.0 slice-start.4
  178.6 6.0 multiply_convert_fusion.3
  184.6 0.0 copy-start.8
  184.6 0.0 copy-start.10
  184.6 0.0 slice-start.5
  184.6 8.7 %fusion.3 = f32[768,2048]{1,0:T(8,128)} fusion(bf16[768,1024]{1,0:T(8,128)(2,1)S(1)} %get-tuple-element.30, bf16[3,2048,1024]{2,1,0:T(8,128)(2,1)} %param.10), kind=kOutput, calls=%fused_computation.16 | convolution fusion | flops 3221225472 | bytes 12058624 | tf_op jit(solution)/shard_map/dot_general | solution.py:67
  193.3 0.0 copy-done.8
  193.3 0.0 slice-done.3
  193.4 5.4 fusion.9
  198.7 1.3 multiply_convert_fusion.5
  200.0 1.1 copy-done.12
  201.2 8.1 %add_add_fusion = f32[768,2048]{1,0:T(8,128)} fusion(f32[768,2048]{1,0:T(8,128)} %fusion.3, f32[768,2048]{1,0:T(8,128)} %fusion.9, bf16[768,1024]{1,0:T(8,128)(2,1)S(1)} %multiply_convert_fusion.5, bf16[3,2048,1024]{2,1,0:T(8,128)(2,1)S(1)} %bitcast.93), kind=kOutput, calls=%fused_computation.9 | convolution fusion | flops 3224371200 | bytes 24641536 | tf_op jit(solution)/shard_map/dot_general | solution.py:67
  209.3 0.0 reduce-scatter.4.cloned.1.call-update
  209.3 0.2 reduce-scatter.6.cloned.1.call-start
  209.6 6.1 convolution_bitcast_fusion.5
  215.7 0.0 copy-start.9
  215.7 3.5 convolution_bitcast_fusion.4
  219.2 3.6 convolution_bitcast_fusion.3
  222.8 8.7 %pad_maximum_fusion = f32[3,2048,1024]{1,2,0:T(8,128)} fusion(f32[1,2048,1024]{1,2,0:T(8,128)S(1)} %convolution_bitcast_fusion.3, f32[1,2048,1024]{1,2,0:T(8,128)S(1)} %convolution_bitcast_fusion.4, f32[1,2048,1024]{1,2,0:T(8,128)S(1)} %convolution_bitcast_fusion.5), kind=kLoop, calls=%fused_computation.1 | loop fusion | flops 12582912 | bytes 50331648 | tf_op jit(solution)/shard_map/stack | solution.py:87
  231.5 0.0 reduce-scatter.6.cloned.1.call-update
  231.5 0.3 reduce-scatter.8.cloned.1.call-start
  231.8 0.0 copy-start.4
  231.8 0.0 copy-start.7
  231.8 6.6 %convolution_bitcast_fusion.1 = f32[1,1024,2048]{2,1,0:T(8,128)S(1)} fusion(bf16[768,2048]{0,1:T(8,128)(2,1)} %bitcast.80, f32[768]{0:T(1024)S(1)} %get-tuple-element.16, f32[768,1024]{1,0:T(8,128)} %copy-done.2), kind=kOutput, calls=%fused_computation.11 | convolution fusion | flops 3229876224 | bytes 14683136 | tf_op jit(solution)/shard_map/dot_general | solution.py:30
  238.4 3.6 convolution_bitcast_fusion
  242.0 3.6 convolution_bitcast_fusion.2
  245.6 8.6 %pad_maximum_fusion.1 = f32[3,1024,2048]{2,1,0:T(8,128)} fusion(f32[1,1024,2048]{2,1,0:T(8,128)S(1)} %convolution_bitcast_fusion, f32[1,1024,2048]{2,1,0:T(8,128)S(1)} %convolution_bitcast_fusion.1, f32[1,1024,2048]{2,1,0:T(8,128)S(1)} %convolution_bitcast_fusion.2), kind=kLoop, calls=%fused_computation.2 | loop fusion | flops 12582912 | bytes 50331648 | tf_op jit(solution)/shard_map/stack | solution.py:88
  254.2 0.0 reduce-scatter.8.cloned.1.call-update
  254.3 1.1 copy-done.1
  255.4 0.4 convolution_bitcast_fusion.6
  255.8 12.8 %psum.23 = f32[512,2]{0,1:T(2,128)} all-reduce(f32[512,2]{0,1:T(2,128)S(1)} %convolution_bitcast_fusion.6), channel_id=1, replica_groups=mesh['dp'=8,'tensor'=4] {'dp'}, use_global_device_ids=true, to_apply=%region_8.9 | all-reduce | flops 1024 | bytes 8192 | tf_op jit(solution)/shard_map/psum | solution.py:85
  268.5 50.0 %reduce-scatter.4.cloned.1.call-done = f32[768,512]{1,0:T(8,128)} async-done(((f32[768,2048]{1,0:T(8,128)}), f32[768,512]{1,0:T(8,128)}) %reduce-scatter.4.cloned.1.call-update) | async-done | bytes 1572880 | tf_op jit(solution)/shard_map/reduce_scatter | solution.py:80
  318.5 3.4 convolution_add_fusion
  321.9 156.8 %reduce-scatter.6.cloned.1.call-done = f32[3,256,1024]{1,2,0:T(8,128)} async-done(((f32[3,2048,1024]{1,2,0:T(8,128)}), f32[3,256,1024]{1,2,0:T(8,128)}) %reduce-scatter.6.cloned.1.call-update) | async-done | bytes 3145744 | tf_op jit(solution)/shard_map/reduce_scatter | solution.py:87
  478.7 3.5 copy.13
  482.2 156.5 %reduce-scatter.8.cloned.1.call-done = f32[3,1024,256]{2,1,0:T(8,128)} async-done(((f32[3,1024,2048]{2,1,0:T(8,128)}), f32[3,1024,256]{2,1,0:T(8,128)}) %reduce-scatter.8.cloned.1.call-update) | async-done | bytes 3145744 | tf_op jit(solution)/shard_map/reduce_scatter | solution.py:88
  (45 shorter events, 0.2 us)
Async XLA Ops:
  7.2 91.1 %copy-start = (bf16[512,2]{0,1:T(2,128)(2,1)S(1)}, bf16[512,2]{0,1:T(2,128)(2,1)}, u32[]{:S(2)}) copy-start(bf16[512,2]{0,1:T(2,128)(2,1)} %param.9) | copy-start | bytes 6148
  7.2 118.2 %all-gather.2.cloned.1.call-start = ((), (), s32[]{:S(2)}) async-start(), calls=%async_computation.3 | async-start | bytes 3932160 | tf_op jit(solution)/shard_map/all_gather | solution.py:39
  7.9 310.6 %reduce-scatter.4.cloned.1.call-start = ((), (), s32[]{:S(2)}) async-start(), calls=%async_computation.4 | async-start | bytes 7864320 | tf_op jit(solution)/shard_map/reduce_scatter | solution.py:80
  8.0 29.8 %collective-permute-start = (bf16[768,512]{1,0:T(8,128)(2,1)}, bf16[768,512]{1,0:T(8,128)(2,1)S(1)}, u32[]{:S(2)}, u32[]{:S(2)}) collective-permute-start(bf16[768,512]{1,0:T(8,128)(2,1)} %param.8), channel_id=1, source_target_pairs={{0,1},{1,2},{2,3},{3,0},{4,5},{5,6},{6,7},{7,4},{8,9},{9,10},{10,1... | collective-permute-start | bytes 2359304 | tf_op jit(solution)/shard_map/ppermute | solution.py:18
  37.8 77.7 %copy-start.13 = (bf16[768,512]{1,0:T(8,128)(2,1)}, bf16[768,512]{1,0:T(8,128)(2,1)S(1)}, u32[]{:S(2)}) copy-start(bf16[768,512]{1,0:T(8,128)(2,1)S(1)} %collective-permute-done) | copy-start | bytes 2359300
  37.8 45.7 %collective-permute-start.1 = (bf16[768,512]{1,0:T(8,128)(2,1)S(1)}, bf16[768,512]{1,0:T(8,128)(2,1)S(1)}, u32[]{:S(2)}, u32[]{:S(2)}) collective-permute-start(bf16[768,512]{1,0:T(8,128)(2,1)S(1)} %collective-permute-done), channel_id=1, source_target_pairs={{0,1},{1,2},{2,3},{3,0},{4,5},{5,6},{6,7},{7,4},{8,9},{9,10},{10,1... | collective-permute-start | bytes 2359304 | tf_op jit(solution)/shard_map/ppermute | solution.py:18
  83.4 32.0 %copy-start.14 = (bf16[768,512]{1,0:T(8,128)(2,1)}, bf16[768,512]{1,0:T(8,128)(2,1)S(1)}, u32[]{:S(2)}) copy-start(bf16[768,512]{1,0:T(8,128)(2,1)S(1)} %collective-permute-done.1) | copy-start | bytes 2359300
  83.5 32.0 %collective-permute-start.2 = (bf16[768,512]{1,0:T(8,128)(2,1)S(1)}, bf16[768,512]{1,0:T(8,128)(2,1)S(1)}, u32[]{:S(2)}, u32[]{:S(2)}) collective-permute-start(bf16[768,512]{1,0:T(8,128)(2,1)S(1)} %collective-permute-done.1), channel_id=1, source_target_pairs={{0,1},{1,2},{2,3},{3,0},{4,5},{5,6},{6,7},{7,4},{8,9},{9,10},{10,1... | collective-permute-start | bytes 2359304 | tf_op jit(solution)/shard_map/ppermute | solution.py:18
  115.4 0.9 copy-start.15
  125.4 6.3 copy-start.6
  131.7 7.8 %copy-start.17 = (bf16[768,2048]{1,0:T(8,128)(2,1)S(1)}, bf16[768,2048]{1,0:T(8,128)(2,1)}, u32[]{:S(2)}) copy-start(bf16[768,2048]{1,0:T(8,128)(2,1)} %all-gather.2.cloned.1.call-done) | copy-start | bytes 9437188
  131.7 13.2 %slice-start = ((s8[12582912]{0:T(1024)(128)(4,1)}), s8[4194304]{0:T(1024)(128)(4,1)S(1)}, s32[]{:S(2)}) async-start(s8[12582912]{0:T(1024)(128)(4,1)} %bitcast.90), calls=%async_computation.7 | async-start | bytes 8388608
  131.7 13.2 %slice-start.1 = ((s8[12582912]{0:T(1024)(128)(4,1)}), s8[4194304]{0:T(1024)(128)(4,1)S(1)}, s32[]{:S(2)}) async-start(s8[12582912]{0:T(1024)(128)(4,1)} %bitcast.90), calls=%async_computation.8 | async-start | bytes 8388608
  139.5 5.4 slice-start.2
  144.9 5.4 copy-start.2
  156.0 5.4 copy-start.3
  156.0 22.4 %copy-start.16 = (s32[768]{0:T(1024)S(1)}, s32[768]{0:T(1024)}, u32[]{:S(2)}) copy-start(s32[768]{0:T(1024)} %param.7) | copy-start | bytes 9220
  178.6 14.8 %slice-start.3 = ((s8[12582912]{0:T(1024)(128)(4,1)}), s8[4194304]{0:T(1024)(128)(4,1)S(1)}, s32[]{:S(2)}) async-start(s8[12582912]{0:T(1024)(128)(4,1)} %bitcast.92), calls=%async_computation.10 | async-start | bytes 8388608
  178.6 14.8 %slice-start.4 = ((s8[12582912]{0:T(1024)(128)(4,1)}), s8[4194304]{0:T(1024)(128)(4,1)S(1)}, s32[]{:S(2)}) async-start(s8[12582912]{0:T(1024)(128)(4,1)} %bitcast.92), calls=%async_computation.11 | async-start | bytes 8388608
  184.6 8.7 %copy-start.8 = (bf16[768,1024]{1,0:T(8,128)(2,1)}, bf16[768,1024]{1,0:T(8,128)(2,1)S(1)}, u32[]{:S(2)}) copy-start(bf16[768,1024]{1,0:T(8,128)(2,1)S(1)} %get-tuple-element.30) | copy-start | bytes 4718596
  184.6 8.7 %copy-start.10 = (bf16[768,1024]{1,0:T(8,128)(2,1)}, bf16[768,1024]{1,0:T(8,128)(2,1)S(1)}, u32[]{:S(2)}) copy-start(bf16[768,1024]{1,0:T(8,128)(2,1)S(1)} %get-tuple-element.31) | copy-start | bytes 4718596
  184.6 8.7 %slice-start.5 = ((s8[12582912]{0:T(1024)(128)(4,1)}), s8[4194304]{0:T(1024)(128)(4,1)S(1)}, s32[]{:S(2)}) async-start(s8[12582912]{0:T(1024)(128)(4,1)} %bitcast.92), calls=%async_computation.12 | async-start | bytes 8388608
  193.4 5.4 copy-start.5
  200.0 1.1 copy-start.12
  209.3 269.3 %reduce-scatter.6.cloned.1.call-start = ((), (), s32[]{:S(2)}) async-start(), calls=%async_computation.5 | async-start | bytes 28311552 | tf_op jit(solution)/shard_map/reduce_scatter | solution.py:87
  209.6 6.1 copy-start.11
  209.6 6.1 copy-start.18
  215.7 3.6 copy-start.9
  231.5 407.2 %reduce-scatter.8.cloned.1.call-start = ((), (), s32[]{:S(2)}) async-start(), calls=%async_computation.6 | async-start | bytes 28311552 | tf_op jit(solution)/shard_map/reduce_scatter | solution.py:88
  231.8 6.6 %copy-start.4 = (f32[768,1024]{1,0:T(8,128)S(1)}, f32[768,1024]{1,0:T(8,128)}, u32[]{:S(2)}) copy-start(f32[768,1024]{1,0:T(8,128)} %copy-done.3) | copy-start | bytes 9437188
  231.8 6.6 %copy-start.7 = (bf16[768,4,512]{0,2,1:T(8,128)(2,1)S(1)}, bf16[768,4,512]{0,2,1:T(8,128)(2,1)}, u32[]{:S(2)}) copy-start(bf16[768,4,512]{0,2,1:T(8,128)(2,1)} %copy.12) | copy-start | bytes 9437188
  254.2 1.1 copy-start.1
Sparse Core Ops, SparseCore 0:
  9.6 89.7 all-gather.1
  209.5 108.9 reduce-scatter.3
  322.1 156.5 reduce-scatter.5
  482.7 155.9 reduce-scatter.7
